TPU v7x, 512 devices: a whole 4x8x8 slice. The times are simulated.
512 devices in a mesh: seq: 16 (over z, core), dp: 8 (over y), mp: 4 (over x).
Axes of the slice: x: 4, y: 8, z: 8, core: 2. Of those that a mesh axis runs over, the one named last changes fastest.
Arguments:
- features: bfloat16 [8, 4096, 8, 512], P('dp', 'seq', None, 'mp'), may hold values from -6 to 6
- key_projection: bfloat16 [8, 4096, 8, 128], P('dp', 'seq'), may hold values from -2 to 2
- query_proj: bfloat16 [8, 4096, 8, 128], P('dp', 'seq'), may hold values from -2 to 2
- step_raw: float32 [8, 4096, 8, 8], P('dp', 'seq', None, 'mp'), may hold values from -3 to 6
- doc_starts: int32 [8, 4096], P('dp', 'seq'), may hold values 0 or 1
- log_rate: float32 [8, 8], P(None, 'mp'), may hold values from -5 to 1
- step_bias: float32 [8, 8], P(None, 'mp'), may hold values from -5 to -2.5
- skip_gain: float32 [8, 8], P(None, 'mp'), may hold values from 0.5 to 1.5
- out_grad: bfloat16 [8, 4096, 8, 512], P('dp', 'seq', None, 'mp'), may hold values from -6 to 6
Outputs:
- mixed_out: bfloat16 [8, 4096, 8, 512], P('dp', 'seq', None, 'mp')
- features_grad: bfloat16 [8, 4096, 8, 512], P('dp', 'seq', None, 'mp')
- key_grad: bfloat16 [8, 4096, 8, 128], P('dp', 'seq', 'mp')
- query_grad: bfloat16 [8, 4096, 8, 128], P('dp', 'seq', 'mp')
- step_grad: float32 [8, 4096, 8, 8], P('dp', 'seq', None, 'mp')
- log_rate_grad: float32 [8, 8], P(None, 'mp')
- step_bias_grad: float32 [8, 8], P(None, 'mp')
- skip_grad: float32 [8, 8], P(None, 'mp')
All inputs are finite; a program needn't handle non-finite values. No bound on the sum of `doc_starts` on one device may be relied on, other than what follows from the above.
Results may differ from a plain program's by a relative error of at most 0.0015.
Values sent between devices are 32-bit elements; how exact they have to be, the bound alone decides.
No kernel may reach another device: no remote copies, remote signals or barrier semaphores. Data moves between devices by JAX's collectives and lax.ppermute only.
A program may use at most 128 MiB of HBM per device.

v0:
```python
import math
import jax
import jax.numpy as jnp
from jax import lax
from jax.sharding import PartitionSpec as P

P_SIZE = 64
triple = lax.Precision.HIGH


def prefix(shard, axis, combine, identity, reverse):
    length, position = (lax.axis_size(axis), lax.axis_index(axis))
    everything = jax.tree.map(lambda part: lax.all_gather(part, axis), shard)
    start = jax.tree.map(
        lambda part, zero: jnp.broadcast_to(jnp.asarray(zero, part.dtype), part.shape),
        shard,
        identity,
    )

    def step(k, before):
        at = length - 1 - k if reverse else k
        reached = at > position if reverse else at < position
        new = combine(before, jax.tree.map(lambda part: part[at], everything))
        return jax.tree.map(lambda a, b: jnp.where(reached, a, b), new, before)

    return lax.fori_loop(0, length, step, start)


def decay_terms(step_raw, doc_starts, log_rate, step_bias):
    step_size = jax.nn.softplus(step_raw + step_bias)
    log_decay = -step_size * jnp.exp(log_rate)
    cumulative = jnp.cumsum(log_decay, axis=1)
    doc_count = jnp.cumsum(doc_starts, axis=1)
    return (step_size, cumulative, doc_count)


def block_forward(
    head_vals, key_vals, query_vals, step_raw, doc_starts, log_rate, step_bias, skip_gain, state_in
):
    step_size, cumulative, doc_count = decay_terms(step_raw, doc_starts, log_rate, step_bias)
    block_len = head_vals.shape[1]
    causal = jnp.arange(block_len)[:, None] >= jnp.arange(block_len)[None, :]
    same_doc = causal[None] & (doc_count[:, :, None] == doc_count[:, None, :])
    doc_mask = same_doc[..., None, None]
    gap_log = cumulative[:, :, None] - cumulative[:, None, :]
    decay_mat = jnp.where(doc_mask, jnp.exp(jnp.where(doc_mask, gap_log, 0.0)), 0.0)
    entry_decay = jnp.where((doc_count == 0)[:, :, None, None], jnp.exp(cumulative), 0.0)
    scores = jnp.einsum("rtgn,rsgn->rtsg", query_vals, key_vals, precision=triple)
    mixing = scores[..., None] * decay_mat * step_size[:, None]
    output = jnp.einsum("rtsgh,rsghp->rtghp", mixing, head_vals, precision=triple)
    output = (
        output
        + jnp.einsum("rtgn,rghpn->rtghp", query_vals, state_in, precision=triple)
        * entry_decay[..., None]
    )
    output = output + skip_gain[..., None] * head_vals
    last_decay = decay_mat[:, -1]
    state_out = state_in * entry_decay[:, -1][..., None, None]
    state_out = state_out + jnp.einsum(
        "rsgh,rsghp,rsgn->rghpn", last_decay * step_size, head_vals, key_vals, precision=triple
    )
    return (output, state_out)


def block_summary(head_vals, key_vals, step_raw, doc_starts, log_rate, step_bias):
    step_size, cumulative, doc_count = decay_terms(step_raw, doc_starts, log_rate, step_bias)
    tail_doc = (doc_count == doc_count[:, -1:])[:, :, None, None]
    last_decay = jnp.where(
        tail_doc, jnp.exp(jnp.where(tail_doc, cumulative[:, -1:] - cumulative, 0.0)), 0.0
    )
    passed_forward = jnp.where(
        (doc_count[:, -1] == 0)[:, None, None], jnp.exp(cumulative[:, -1]), 0.0
    )
    summary_state = jnp.einsum(
        "rsgh,rsghp,rsgn->rghpn", last_decay * step_size, head_vals, key_vals, precision=triple
    )
    return (passed_forward, summary_state)


def forward_combine(earlier, trailing_portion):
    return (
        earlier[0] * trailing_portion[0],
        trailing_portion[0][..., None, None] * earlier[1] + trailing_portion[1],
    )


def backward_combine(earlier, trailing_portion):
    return (
        earlier[0] * trailing_portion[0],
        trailing_portion[1] + trailing_portion[0][..., None, None] * earlier[1],
    )


def local(
    features,
    key_projection,
    query_proj,
    step_raw,
    doc_starts,
    log_rate,
    step_bias,
    skip_gain,
    out_grad,
):
    row_count, length, groups, feat_width = features.shape
    head_count = feat_width // P_SIZE
    block_len = math.gcd(length, 128)
    block_count = length // block_len
    head_vals = features.astype(jnp.float32).reshape(row_count, length, groups, head_count, P_SIZE)
    key_vals = key_projection.astype(jnp.float32)
    query_vals = query_proj.astype(jnp.float32)
    passed_forward, summary_state = block_summary(
        head_vals, key_vals, step_raw, doc_starts, log_rate, step_bias
    )
    state_in = prefix(
        (passed_forward, summary_state),
        "seq",
        forward_combine,
        (jnp.ones_like(passed_forward), jnp.zeros_like(summary_state)),
        False,
    )[1]

    def to_blocks(array):
        return jnp.moveaxis(
            array.reshape((row_count, block_count, block_len) + array.shape[2:]), 1, 0
        )

    def local_layer(
        head_vals, key_vals, query_vals, step_raw, log_rate, step_bias, skip_gain, state_in
    ):

        def stepper(state, pieces):
            vals_b, keys_b, queries_b, raw_b, starts_b = pieces
            output, new_state = block_forward(
                vals_b, keys_b, queries_b, raw_b, starts_b, log_rate, step_bias, skip_gain, state
            )
            return (new_state, output)

        final_state, block_outs = lax.scan(
            jax.checkpoint(stepper),
            state_in,
            (
                to_blocks(head_vals),
                to_blocks(key_vals),
                to_blocks(query_vals),
                to_blocks(step_raw),
                to_blocks(doc_starts),
            ),
        )
        outputs = jnp.moveaxis(block_outs, 0, 1).reshape(
            row_count, length, groups, head_count, P_SIZE
        )
        return (outputs, final_state)

    primal, pullback = jax.vjp(
        local_layer,
        head_vals,
        key_vals,
        query_vals,
        step_raw,
        log_rate,
        step_bias,
        skip_gain,
        state_in,
    )
    mixed_vals = primal[0]
    cotangent = out_grad.astype(jnp.float32).reshape(head_vals.shape)
    _, cumulative, doc_count = decay_terms(step_raw, doc_starts, log_rate, step_bias)
    entry_decay = jnp.where((doc_count == 0)[:, :, None, None], jnp.exp(cumulative), 0.0)
    adjoint_local = jnp.einsum(
        "rtgh,rtghp,rtgn->rghpn", entry_decay, cotangent, query_vals, precision=triple
    )
    adjoint_in = prefix(
        (passed_forward, adjoint_local),
        "seq",
        backward_combine,
        (jnp.ones_like(passed_forward), jnp.zeros_like(adjoint_local)),
        True,
    )[1]
    gradients = pullback((cotangent, adjoint_in))
    vals_grad, keys_grad, queries_grad, raw_grad, rate_grad, bias_grad, gain_grad, _ = gradients
    key_part, query_part = (
        lax.psum_scatter(keys_grad, "mp", scatter_dimension=2, tiled=True),
        lax.psum_scatter(queries_grad, "mp", scatter_dimension=2, tiled=True),
    )
    rate_total, bias_total, gain_total = lax.psum((rate_grad, bias_grad, gain_grad), ("seq", "dp"))
    return (
        mixed_vals.reshape(features.shape).astype(jnp.bfloat16),
        vals_grad.reshape(features.shape).astype(jnp.bfloat16),
        key_part.astype(jnp.bfloat16),
        query_part.astype(jnp.bfloat16),
        raw_grad,
        rate_total,
        bias_total,
        gain_total,
    )


def solution(mesh):
    return jax.shard_map(
        local,
        mesh=mesh,
        in_specs=(
            P("dp", "seq", None, "mp"),
            P("dp", "seq", None, None),
            P("dp", "seq", None, None),
            P("dp", "seq", None, "mp"),
            P("dp", "seq"),
            P(None, "mp"),
            P(None, "mp"),
            P(None, "mp"),
            P("dp", "seq", None, "mp"),
        ),
        out_specs=(
            P("dp", "seq", None, "mp"),
            P("dp", "seq", None, "mp"),
            P("dp", "seq", "mp", None),
            P("dp", "seq", "mp", None),
            P("dp", "seq", None, "mp"),
            P(None, "mp"),
            P(None, "mp"),
            P(None, "mp"),
        ),
        check_vma=False,
    )
```

profile of v0, /device:TPU:2, one launch (start us, length us, event | category | flops | bytes accessed | tf_op | source)
XLA Modules:
  0.0 560.6 jit_solution(17976242943628089828)
XLA Ops:
  15.7 2.3 fusion.127
  24.7 2.1 copy.470
  26.8 2.1 copy.469
  30.1 23.6 %all_gather.18 = f32[16,1,8,2]{2,3,1,0:T(2,128)S(1)} all-gather(f32[1,1,8,2]{2,3,1,0:T(2,128)S(1)} %copy.462), channel_id=1, replica_groups=mesh['seq'=16,'dp'=8,'mp'=4] {'seq'}, dimensions={0}, use_global_device_ids=true | all-gather | bytes 1088 | tf_op jit(solution)/shard_map/all_gather | solution.py:13
  53.7 28.4 %all-gather.7.cloned.1.call-done = f32[128,2,64,128]{3,2,1,0:T(8,128)} async-done(((f32[8,2,64,128]{3,2,1,0:T(8,128)}), f32[128,2,64,128]{3,2,1,0:T(8,128)}) %all-gather.7.cloned.1.call-update) | async-done | bytes 8388624 | tf_op jit(solution)/shard_map/all_gather | solution.py:13
  82.1 20.8 %while.78 = (s32[]{:T(128)}, f32[1,8,2,64,128]{4,3,2,1,0:T(8,128)S(1)}, s32[]{:T(128)}, f32[16,1,8,2,64,128]{5,4,3,2,1,0:T(8,128)}, f32[16,1,8,2]{2,3,1,0:T(2,12...) while((s32[]{:T(128)}, f32[1,8,2,64,128]{4,3,2,1,0:T(8,128)S(1)}, s32[]{:T(128)}, ...), condition=%wide.region_11.12_spmd.clone, body=%wide.region_10.11_spmd.clone.sunk | while | flops 524296 | bytes 1573359 | solution.py:26
  102.9 39.2 %all-gather.5.cloned.1.call-done = f32[128,2,64,128]{3,2,1,0:T(8,128)} async-done(((f32[8,2,64,128]{3,2,1,0:T(8,128)}), f32[128,2,64,128]{3,2,1,0:T(8,128)}) %all-gather.5.cloned.1.call-update) | async-done | bytes 8388624 | tf_op jit(solution)/shard_map/all_gather | solution.py:13
  142.1 20.6 %while.77 = (s32[]{:T(128)}, f32[1,8,2,64,128]{4,3,2,1,0:T(8,128)S(1)}, s32[]{:T(128)}, f32[16,1,8,2]{2,3,1,0:T(2,128)S(1)}, f32[16,1,8,2,64,128]{5,4,3,2,1,0:T(8,128)}, /*index=5*/s32[]{:T(128)}, s32[]{:T(128)}) while((s32[]{:T(128)}, f32[1,8,2,64,128]{4,3,2,1,0:T(8,128)S(1)}, s32[]{:T(128)}, f32[16,1,8,2]{2,3,1,0:T(2,128)S(1)}, ...), condition=%wide.region_5.6_spmd.clone, body=%wide.region_4.5_spmd.clone.sunk | while | flops 524292 | bytes 1573297 | solution.py:26
  163.7 30.4 %while.76 = (s32[]{:T(128)}, f32[1,8,2,64,128]{4,3,2,1,0:T(8,128)S(1)}, bf16[2,1,128,8,2,64]{2,5,4,3,1,0:T(8,128)(2,1)}, f32[2,1,8,2,64,128]{5,4,3,2,1,0:T(8,128...) while((s32[]{:T(128)}, ...), condition=%wide.region_9.10_spmd.clone, body=%wide.region_6.9_spmd.clone.sunk | while | flops 405264384 | bytes 14427908 | solution.py:139
  173.2 3.3 fusion.211
  188.4 3.3 fusion.211
  197.8 90.8 %while.79 = (s32[]{:T(128)}, f32[8,2]{1,0:T(8,128)}, f32[8,2]{0,1:T(2,128)}, f32[8,2]{1,0:T(8,128)}, f32[1,8,2,64,128]{4,3,2,1,0:T(8,128)S(1)}, /*index=5*/bf16[...) while((s32[]{:T(128)}, f32[8,2]{1,0:T(8,128)}, ...), condition=%wide.region_25.26_spmd.clone, body=%wide.region_12.25_spmd.clone.sunk | while | flops 1015154816 | bytes 36794436 | solution.py:139
  208.9 2.0 copy.623
  210.9 2.0 copy.612
  223.2 3.3 fusion.239
  229.7 1.9 fusion.242
  235.7 2.7 fusion.245
  254.3 2.0 copy.623
  256.3 2.0 copy.612
  268.6 3.3 fusion.239
  281.7 2.7 fusion.245
  290.7 250.9 %all-reduce.2 = (f32[8,2]{0,1:T(2,128)}, f32[8,2]{0,1:T(2,128)}, f32[8,2]{0,1:T(2,128)}) all-reduce(f32[8,2]{0,1:T(2,128)} %get-tuple-element.780, f32[8,2]{0,1:T(2,128)S(1)} %copy.487, f32[8,2]{0,1:T(2,128)S(1)} %copy.488), channel_id=1, replica_groups=mesh['seq'=16,'dp'=8,'mp'=4] {'seq','dp'}, use_global_device_ids=true, to_apply=%region_28.29 | all-reduce | flops 48 | bytes 384 | tf_op jit(solution)/shard_map/psum | solution.py:186
  543.0 2.5 copy.509
  546.8 2.5 copy.512
  (334 shorter events, 161.4 us)
Async XLA Ops:
  7.2 14.6 %copy-start.4 = (f32[1,256,8,2]{1,3,2,0:T(2,128)S(1)}, f32[1,256,8,2]{1,3,2,0:T(2,128)}, u32[]{:S(2)}) copy-start(f32[1,256,8,2]{1,3,2,0:T(2,128)} %param.20) | copy-start | bytes 49156
  7.2 13.3 %copy-start.2 = (bf16[1,256,8,128]{3,2,1,0:T(8,128)(2,1)S(1)}, bf16[1,256,8,128]{3,2,1,0:T(8,128)(2,1)}, u32[]{:S(2)}) copy-start(bf16[1,256,8,128]{3,2,1,0:T(8,128)(2,1)} %param.18) | copy-start | bytes 1572868
  7.2 16.7 %copy-start.6 = (f32[8,2]{0,1:T(2,128)S(1)}, f32[8,2]{0,1:T(2,128)}, u32[]{:S(2)}) copy-start(f32[8,2]{0,1:T(2,128)} %param.24) | copy-start | bytes 196
  7.2 74.9 %all-gather.7.cloned.1.call-start = ((), (), s32[]{:S(2)}) async-start(), calls=%async_computation.5 | async-start | bytes 8912896 | tf_op jit(solution)/shard_map/all_gather | solution.py:13
  18.0 124.2 %all-gather.5.cloned.1.call-start = ((), (), s32[]{:S(2)}) async-start(), calls=%async_computation.4 | async-start | bytes 8912896 | tf_op jit(solution)/shard_map/all_gather | solution.py:13
  21.7 528.9 %reduce-scatter.5.cloned.1.call-start = ((), (), s32[]{:S(2)}) async-start(), calls=%async_computation.3 | async-start | bytes 1310720 | tf_op jit(solution)/shard_map/reduce_scatter | solution.py:184
  82.1 81.6 %copy-start.3 = (f32[8,2]{0,1:T(2,128)S(1)}, f32[8,2]{0,1:T(2,128)}, u32[]{:S(2)}) copy-start(f32[8,2]{0,1:T(2,128)} %param.23) | copy-start | bytes 196
  168.5 8.8 %copy-start.1 = (f32[2,1,128,8,2,64]{2,5,4,3,1,0:T(8,128)S(1)}, f32[2,1,128,8,2,64]{2,5,4,3,1,0:T(8,128)}, u32[]{:S(2)}) copy-start(f32[2,1,128,8,2,64]{2,5,4,3,1,0:T(8,128)} %get-tuple-element.1742) | copy-start | bytes 3145732 | tf_op jit(solution)/shard_map/jvp()/while
  183.7 8.8 %copy-start.1 = (f32[2,1,128,8,2,64]{2,5,4,3,1,0:T(8,128)S(1)}, f32[2,1,128,8,2,64]{2,5,4,3,1,0:T(8,128)}, u32[]{:S(2)}) copy-start(f32[2,1,128,8,2,64]{2,5,4,3,1,0:T(8,128)} %get-tuple-element.1742) | copy-start | bytes 3145732 | tf_op jit(solution)/shard_map/jvp()/while
  202.4 12.1 %copy-start = (f32[1,8,2,64,128]{4,3,2,1,0:T(8,128)}, f32[1,8,2,64,128]{4,3,2,1,0:T(8,128)S(1)}, u32[]{:S(2)}) copy-start(f32[1,8,2,64,128]{4,3,2,1,0:T(8,128)S(1)} %dynamic-slice_bitcast_fusion.17) | copy-start | bytes 1572868 | tf_op jit(solution)/shard_map/transpose(jvp())/while
  206.7 15.4 %copy-start.5 = (pred[128]{0:T(512)(128)(4,1)}, pred[128]{0:T(512)(128)(4,1)S(1)}, u32[]{:S(2)}) copy-start(pred[128]{0:T(512)(128)(4,1)S(1)} %broadcast_compare_fusion.5) | copy-start | bytes 388 | tf_op jit(solution)/shard_map/transpose(jvp())/while
  247.2 12.8 %copy-start = (f32[1,8,2,64,128]{4,3,2,1,0:T(8,128)}, f32[1,8,2,64,128]{4,3,2,1,0:T(8,128)S(1)}, u32[]{:S(2)}) copy-start(f32[1,8,2,64,128]{4,3,2,1,0:T(8,128)S(1)} %dynamic-slice_bitcast_fusion.17) | copy-start | bytes 1572868 | tf_op jit(solution)/shard_map/transpose(jvp())/while
  252.1 15.4 %copy-start.5 = (pred[128]{0:T(512)(128)(4,1)}, pred[128]{0:T(512)(128)(4,1)S(1)}, u32[]{:S(2)}) copy-start(pred[128]{0:T(512)(128)(4,1)S(1)} %broadcast_compare_fusion.5) | copy-start | bytes 388 | tf_op jit(solution)/shard_map/transpose(jvp())/while
  288.6 263.7 %reduce-scatter.3.cloned.1.call-start = ((), (), s32[]{:S(2)}) async-start(), calls=%async_computation.2 | async-start | bytes 1310720 | tf_op jit(solution)/shard_map/reduce_scatter | solution.py:183
Sparse Core Ops, SparseCore 0:
  18.1 63.9 all-gather.6
  84.8 57.2 all-gather.4
  288.7 24.6 reduce-scatter.4
  316.2 28.8 reduce-scatter.2
where the time goes:
time: 565 us; the launch traced here: 561 us
  blocking collectives  275 us (49%)
  local copies, waits for them, and re-layouts  81.3 us (14%)
  other arithmetic  75.2 us (13%)
  waiting for transfers between devices  68.2 us (12%)
  matrix products  44.3 us (8%)
  between operations  15.3 us (3%)
    psum x1, blocking collectives, local(): lax.psum((rate_grad, bias_grad, gain_grad), ('seq', 'dp'))  251 us
    all_gather x2, waiting for transfers between devices, prefix(): everything = jax.tree.map(lambda part: lax.all_gather(part, axis), shard)  67.6 us
    select_n x32, other arithmetic, step(): return jax.tree.map(lambda a, b: jnp.where(reached, a, b), new, before)  37.5 us
    all_gather x1, blocking collectives, prefix(): everything = jax.tree.map(lambda part: lax.all_gather(part, axis), shard)  23.6 us
    unnamed x21, local copies, waits for them, and re-layouts  17.9 us
    dot_general x6, matrix products, block_forward(): jnp.einsum('rtsgh,rsghp->rtghp', mixing, head_vals, precision=triple)  14 us
  transfers between devices with their start and end apart: 4, of which 2 were waited for; matrix products, arithmetic and copies ran while one was open for 8% of the time, Pallas kernels for 0%

commit v1 on v0

--- a/solution.py
+++ b/solution.py
@@ -102,6 +102,12 @@
     skip_gain,
     out_grad,
 ):
+
+    def _drive_joints(xin):
+        for t in ("seq", "dp"):
+            xin = lax.psum(xin, t)
+        return xin
+
     row_count, length, groups, feat_width = features.shape
     head_count = feat_width // P_SIZE
     block_len = math.gcd(length, 128)
@@ -183,7 +189,7 @@
         lax.psum_scatter(keys_grad, "mp", scatter_dimension=2, tiled=True),
         lax.psum_scatter(queries_grad, "mp", scatter_dimension=2, tiled=True),
     )
-    rate_total, bias_total, gain_total = lax.psum((rate_grad, bias_grad, gain_grad), ("seq", "dp"))
+    rate_total, bias_total, gain_total = _drive_joints((rate_grad, bias_grad, gain_grad))
     return (
         mixed_vals.reshape(features.shape).astype(jnp.bfloat16),
         vals_grad.reshape(features.shape).astype(jnp.bfloat16),

time: 565 us -> 360 us (0.64)
  the two profiles are of different devices: /device:TPU:2 before, /device:TPU:8 now
where the time goes in v1:
time: 360 us; the launch traced here: 356 us
  local copies, waits for them, and re-layouts  81.3 us (23%)
  other arithmetic  75.2 us (21%)
  waiting for transfers between devices  72.6 us (20%)
  blocking collectives  65.1 us (18%)
  matrix products  44.3 us (12%)
  between operations  15.3 us (4%)
    all_gather x2, waiting for transfers between devices, prefix(): everything = jax.tree.map(lambda part: lax.all_gather(part, axis), shard)  67.5 us
    psum x2, blocking collectives, _drive_joints(): xin = lax.psum(xin, t)  41.5 us
    select_n x32, other arithmetic, step(): return jax.tree.map(lambda a, b: jnp.where(reached, a, b), new, before)  37.5 us
    all_gather x1, blocking collectives, prefix(): everything = jax.tree.map(lambda part: lax.all_gather(part, axis), shard)  23.6 us
    unnamed x23, local copies, waits for them, and re-layouts  17.9 us
    dot_general x6, matrix products, block_forward(): jnp.einsum('rtsgh,rsghp->rtghp', mixing, head_vals, precision=triple)  14 us
    dot_general x8, matrix products, block_forward(): jnp.einsum('rtgn,rsgn->rtsg', query_vals, key_vals, precision=triple)  10.4 us
    mul x10, local copies, waits for them, and re-layouts, block_forward(): mixing = scores[..., None] * decay_mat * step_size[:, None]  10.2 us
  transfers between devices with their start and end apart: 4, of which 3 were waited for; matrix products, arithmetic and copies ran while one was open for 12% of the time, Pallas kernels for 0%

profile of v1, /device:TPU:8, one launch (start us, length us, event | category | flops | bytes accessed | tf_op | source)
XLA Modules:
  0.0 355.7 jit_solution(3272531039260423616)
XLA Ops:
  15.7 2.3 fusion.127
  24.7 2.1 copy.470
  26.8 2.1 copy.469
  30.1 23.6 %all_gather.18 = f32[16,1,8,2]{2,3,1,0:T(2,128)S(1)} all-gather(f32[1,1,8,2]{2,3,1,0:T(2,128)S(1)} %copy.462), channel_id=1, replica_groups=mesh['seq'=16,'dp'=8,'mp'=4] {'seq'}, dimensions={0}, use_global_device_ids=true | all-gather | bytes 1088 | tf_op jit(solution)/shard_map/all_gather | solution.py:13
  53.7 28.3 %all-gather.7.cloned.1.call-done = f32[128,2,64,128]{3,2,1,0:T(8,128)} async-done(((f32[8,2,64,128]{3,2,1,0:T(8,128)}), f32[128,2,64,128]{3,2,1,0:T(8,128)}) %all-gather.7.cloned.1.call-update) | async-done | bytes 8388624 | tf_op jit(solution)/shard_map/all_gather | solution.py:13
  82.0 20.8 %while.78 = (s32[]{:T(128)}, f32[1,8,2,64,128]{4,3,2,1,0:T(8,128)S(1)}, s32[]{:T(128)}, f32[16,1,8,2,64,128]{5,4,3,2,1,0:T(8,128)}, f32[16,1,8,2]{2,3,1,0:T(2,12...) while((s32[]{:T(128)}, f32[1,8,2,64,128]{4,3,2,1,0:T(8,128)S(1)}, s32[]{:T(128)}, ...), condition=%wide.region_11.12_spmd.clone, body=%wide.region_10.11_spmd.clone.sunk | while | flops 524296 | bytes 1573359 | solution.py:26
  102.9 39.2 %all-gather.5.cloned.1.call-done = f32[128,2,64,128]{3,2,1,0:T(8,128)} async-done(((f32[8,2,64,128]{3,2,1,0:T(8,128)}), f32[128,2,64,128]{3,2,1,0:T(8,128)}) %all-gather.5.cloned.1.call-update) | async-done | bytes 8388624 | tf_op jit(solution)/shard_map/all_gather | solution.py:13
  142.0 20.6 %while.77 = (s32[]{:T(128)}, f32[1,8,2,64,128]{4,3,2,1,0:T(8,128)S(1)}, s32[]{:T(128)}, f32[16,1,8,2]{2,3,1,0:T(2,128)S(1)}, f32[16,1,8,2,64,128]{5,4,3,2,1,0:T(8,128)}, /*index=5*/s32[]{:T(128)}, s32[]{:T(128)}) while((s32[]{:T(128)}, f32[1,8,2,64,128]{4,3,2,1,0:T(8,128)S(1)}, s32[]{:T(128)}, f32[16,1,8,2]{2,3,1,0:T(2,128)S(1)}, ...), condition=%wide.region_5.6_spmd.clone, body=%wide.region_4.5_spmd.clone.sunk | while | flops 524292 | bytes 1573297 | solution.py:26
  163.6 30.4 %while.76 = (s32[]{:T(128)}, f32[1,8,2,64,128]{4,3,2,1,0:T(8,128)S(1)}, bf16[2,1,128,8,2,64]{2,5,4,3,1,0:T(8,128)(2,1)}, f32[2,1,8,2,64,128]{5,4,3,2,1,0:T(8,128...) while((s32[]{:T(128)}, ...), condition=%wide.region_9.10_spmd.clone, body=%wide.region_6.9_spmd.clone.sunk | while | flops 405264384 | bytes 14427908 | solution.py:145
  173.1 3.3 fusion.211
  188.3 3.3 fusion.211
  197.8 90.8 %while.79 = (s32[]{:T(128)}, f32[8,2]{1,0:T(8,128)}, f32[8,2]{0,1:T(2,128)}, f32[8,2]{1,0:T(8,128)}, f32[1,8,2,64,128]{4,3,2,1,0:T(8,128)S(1)}, /*index=5*/bf16[...) while((s32[]{:T(128)}, f32[8,2]{1,0:T(8,128)}, ...), condition=%wide.region_25.26_spmd.clone, body=%wide.region_12.25_spmd.clone.sunk | while | flops 1015154816 | bytes 36794436 | solution.py:145
  210.8 2.0 copy.612
  223.1 3.3 fusion.239
  235.6 2.7 fusion.245
  254.2 2.0 copy.623
  256.3 2.0 copy.612
  268.5 3.3 fusion.239
  281.7 2.7 fusion.245
  292.0 2.5 copy.509
  295.8 2.5 copy.512
  299.6 25.3 %all-reduce.2 = (f32[8,2]{0,1:T(2,128)S(1)}, f32[8,2]{0,1:T(2,128)S(1)}, f32[8,2]{0,1:T(2,128)S(1)}) all-reduce(f32[8,2]{0,1:T(2,128)S(1)} %copy-done.7, f32[8,2]{0,1:T(2,128)S(1)} %copy.487, f32[8,2]{0,1:T(2,128)S(1)} %copy.488), channel_id=1, replica_groups=mesh['seq'=16,'dp'=8,'mp'=4] {'seq'}, use_global_device_ids=true, to_apply=%region_28.29 | all-reduce | flops 48 | bytes 384 | tf_op jit(solution)/shard_map/psum | solution.py:108
  324.8 16.2 %all-reduce.3 = (f32[8,2]{0,1:T(2,128)}, f32[8,2]{0,1:T(2,128)}, f32[8,2]{0,1:T(2,128)}) all-reduce(f32[8,2]{0,1:T(2,128)S(1)} %get-tuple-element.1337, f32[8,2]{0,1:T(2,128)S(1)} %get-tuple-element.1338, f32[8,2]{0,1:T(2,128)S(1)} %get-tuple-element.1339), channel_id=1, replica_groups=mesh['seq'=16,'dp'=8,'mp'=4] {'dp'}, use_global_device_ids=true, to_apply=%region_29.30 | all-reduce | flops 48 | bytes 384 | tf_op jit(solution)/shard_map/psum | solution.py:108
  342.8 4.5 %reduce-scatter.3.cloned.1.call-done = f32[1,256,2,128]{3,1,0,2:T(8,128)} async-done(((f32[1,256,8,128]{3,1,0,2:T(8,128)}), f32[1,256,2,128]{3,1,0,2:T(8,128)}) %reduce-scatter.3.cloned.1.call-update) | async-done | bytes 262160 | tf_op jit(solution)/shard_map/reduce_scatter | solution.py:189
  (337 shorter events, 165.3 us)
Async XLA Ops:
  7.2 14.6 %copy-start.4 = (f32[1,256,8,2]{1,3,2,0:T(2,128)S(1)}, f32[1,256,8,2]{1,3,2,0:T(2,128)}, u32[]{:S(2)}) copy-start(f32[1,256,8,2]{1,3,2,0:T(2,128)} %param.20) | copy-start | bytes 49156
  7.2 13.3 %copy-start.2 = (bf16[1,256,8,128]{3,2,1,0:T(8,128)(2,1)S(1)}, bf16[1,256,8,128]{3,2,1,0:T(8,128)(2,1)}, u32[]{:S(2)}) copy-start(bf16[1,256,8,128]{3,2,1,0:T(8,128)(2,1)} %param.18) | copy-start | bytes 1572868
  7.2 16.7 %copy-start.6 = (f32[8,2]{0,1:T(2,128)S(1)}, f32[8,2]{0,1:T(2,128)}, u32[]{:S(2)}) copy-start(f32[8,2]{0,1:T(2,128)} %param.24) | copy-start | bytes 196
  7.2 74.8 %all-gather.7.cloned.1.call-start = ((), (), s32[]{:S(2)}) async-start(), calls=%async_computation.5 | async-start | bytes 8912896 | tf_op jit(solution)/shard_map/all_gather | solution.py:13
  18.0 124.1 %all-gather.5.cloned.1.call-start = ((), (), s32[]{:S(2)}) async-start(), calls=%async_computation.4 | async-start | bytes 8912896 | tf_op jit(solution)/shard_map/all_gather | solution.py:13
  21.7 319.4 %reduce-scatter.5.cloned.1.call-start = ((), (), s32[]{:S(2)}) async-start(), calls=%async_computation.3 | async-start | bytes 1310720 | tf_op jit(solution)/shard_map/reduce_scatter | solution.py:190
  82.0 81.6 %copy-start.3 = (f32[8,2]{0,1:T(2,128)S(1)}, f32[8,2]{0,1:T(2,128)}, u32[]{:S(2)}) copy-start(f32[8,2]{0,1:T(2,128)} %param.23) | copy-start | bytes 196
  168.4 8.8 %copy-start.1 = (f32[2,1,128,8,2,64]{2,5,4,3,1,0:T(8,128)S(1)}, f32[2,1,128,8,2,64]{2,5,4,3,1,0:T(8,128)}, u32[]{:S(2)}) copy-start(f32[2,1,128,8,2,64]{2,5,4,3,1,0:T(8,128)} %get-tuple-element.1745) | copy-start | bytes 3145732 | tf_op jit(solution)/shard_map/jvp()/while
  183.6 8.8 %copy-start.1 = (f32[2,1,128,8,2,64]{2,5,4,3,1,0:T(8,128)S(1)}, f32[2,1,128,8,2,64]{2,5,4,3,1,0:T(8,128)}, u32[]{:S(2)}) copy-start(f32[2,1,128,8,2,64]{2,5,4,3,1,0:T(8,128)} %get-tuple-element.1745) | copy-start | bytes 3145732 | tf_op jit(solution)/shard_map/jvp()/while
  202.4 12.1 %copy-start = (f32[1,8,2,64,128]{4,3,2,1,0:T(8,128)}, f32[1,8,2,64,128]{4,3,2,1,0:T(8,128)S(1)}, u32[]{:S(2)}) copy-start(f32[1,8,2,64,128]{4,3,2,1,0:T(8,128)S(1)} %dynamic-slice_bitcast_fusion.17) | copy-start | bytes 1572868 | tf_op jit(solution)/shard_map/transpose(jvp())/while
  206.7 15.4 %copy-start.5 = (pred[128]{0:T(512)(128)(4,1)}, pred[128]{0:T(512)(128)(4,1)S(1)}, u32[]{:S(2)}) copy-start(pred[128]{0:T(512)(128)(4,1)S(1)} %broadcast_compare_fusion.5) | copy-start | bytes 388 | tf_op jit(solution)/shard_map/transpose(jvp())/while
  247.1 12.8 %copy-start = (f32[1,8,2,64,128]{4,3,2,1,0:T(8,128)}, f32[1,8,2,64,128]{4,3,2,1,0:T(8,128)S(1)}, u32[]{:S(2)}) copy-start(f32[1,8,2,64,128]{4,3,2,1,0:T(8,128)S(1)} %dynamic-slice_bitcast_fusion.17) | copy-start | bytes 1572868 | tf_op jit(solution)/shard_map/transpose(jvp())/while
  252.1 15.4 %copy-start.5 = (pred[128]{0:T(512)(128)(4,1)}, pred[128]{0:T(512)(128)(4,1)S(1)}, u32[]{:S(2)}) copy-start(pred[128]{0:T(512)(128)(4,1)S(1)} %broadcast_compare_fusion.5) | copy-start | bytes 388 | tf_op jit(solution)/shard_map/transpose(jvp())/while
  288.5 11.0 %copy-start.7 = (f32[8,2]{0,1:T(2,128)S(1)}, f32[8,2]{0,1:T(2,128)}, u32[]{:S(2)}) copy-start(f32[8,2]{0,1:T(2,128)} %get-tuple-element.780) | copy-start | bytes 196
  288.6 58.8 %reduce-scatter.3.cloned.1.call-start = ((), (), s32[]{:S(2)}) async-start(), calls=%async_computation.2 | async-start | bytes 1310720 | tf_op jit(solution)/shard_map/reduce_scatter | solution.py:189
Sparse Core Ops, SparseCore 0:
  18.1 63.9 all-gather.6
  84.7 57.2 all-gather.4
  288.7 27.1 reduce-scatter.4
  318.6 28.7 reduce-scatter.2
